TPU v7x, 32 devices: a whole 2x2x4 slice. The times are simulated.
32 devices in a mesh: pipe: 2 (over core), expert: 16 (over z, y, x).
Axes of the slice: x: 2, y: 2, z: 4, core: 2. Of those that a mesh axis runs over, the one named last changes fastest.
Arguments:
- tokens: bfloat16 [4096, 2048], P(('pipe', 'expert')), may hold values from -6 to 6
- routes: int32 [4096, 8], P(('pipe', 'expert')), may hold values from 0 to 15, all different within a row; in each aligned block of 128 rows (0 to 127, 128 to 255, ...) at most 64 rows name the same one
- gates: float32 [4096, 8], P(('pipe', 'expert')), may hold values from 0.1 to 1
- cotangent: bfloat16 [4096, 2048], P(('pipe', 'expert')), may hold values from -1.5 to 1.5
- w_gate: bfloat16 [16, 2048, 384], P('expert'), may hold values from -0.125 to 0.125
- w_up: bfloat16 [16, 2048, 384], P('expert'), may hold values from -0.125 to 0.125
- w_down: bfloat16 [16, 384, 2048], P('expert'), may hold values from -0.3125 to 0.3125
Outputs:
- mixed: bfloat16 [4096, 2048], P(('pipe', 'expert'))
- input_grad: bfloat16 [4096, 2048], P(('pipe', 'expert'))
- gate_weight_grad: bfloat16 [16, 2048, 384], P('expert')
- up_weight_grad: bfloat16 [16, 2048, 384], P('expert')
- down_weight_grad: bfloat16 [16, 384, 2048], P('expert')
Inputs may be any that keep to these rules, and one draw needn't show every extreme that they name: `routes`: each row names 8 different experts. Within the rows of one device (aligned blocks of 128 rows, device order pipe then expert) each expert is named exactly 64 times.
All inputs are finite; a program needn't handle non-finite values.
Results may differ from a plain program's by a relative error of at most 0.009.
Values may be sent and summed in bfloat16 or wider, within the bound.
No kernel may reach another device: no remote copies, remote signals or barrier semaphores. Data moves between devices by JAX's collectives and lax.ppermute only.
A program may use at most 128 MiB of HBM per device.

v0:
```python
import jax
import jax.numpy as jnp
from jax import lax
from jax.sharding import PartitionSpec as P


def slot_index(block_routes, expert_count, capacity):
    flat = block_routes.reshape(-1)
    onehot = (flat[:, None] == jnp.arange(expert_count, dtype=jnp.int32)[None, :]).astype(jnp.int32)
    before = jnp.cumsum(onehot, axis=0) - onehot
    ranks = jnp.sum(before * onehot, axis=1)
    return flat * capacity + ranks


def expert_forward(block, gate_mat, up_mat, down_mat):
    inputs = block.reshape(-1, block.shape[2])
    gate_pre = jnp.dot(inputs, gate_mat, preferred_element_type=jnp.float32)
    up_pre = jnp.dot(inputs, up_mat, preferred_element_type=jnp.float32)
    sigma = jax.nn.sigmoid(gate_pre)
    hidden = (gate_pre * sigma * up_pre).astype(jnp.bfloat16)
    outputs = jnp.dot(hidden, down_mat, preferred_element_type=jnp.float32).astype(jnp.bfloat16)
    return (gate_pre, up_pre, hidden, outputs)


def on_device(tokens, routes, gates, cotangent, w_gate, w_up, w_down):
    rows_dev, width = tokens.shape
    picks = routes.shape[1]
    experts = lax.axis_size("expert")
    capacity = rows_dev * picks // experts
    gate_mat = w_gate[0]
    up_mat = w_up[0]
    down_mat = w_down[0]
    inner = gate_mat.shape[1]
    slots = slot_index(routes, experts, capacity)
    flat_rows = jnp.arange(rows_dev * picks, dtype=jnp.int32) // picks
    token_of = jnp.full((experts * capacity,), rows_dev, jnp.int32).at[slots].set(flat_rows)
    weight_of = jnp.zeros((experts * capacity,), jnp.float32).at[slots].set(gates.reshape(-1))
    token_pad = jnp.concatenate([tokens, jnp.zeros((1, width), tokens.dtype)], axis=0)
    send = token_pad[token_of].reshape(experts, capacity, width)
    block = lax.all_to_all(send, "expert", split_axis=0, concat_axis=0, tiled=True)
    items = block.shape[1]
    gate_pre, up_pre, hidden, outputs = expert_forward(block, gate_mat, up_mat, down_mat)
    back_items = lax.all_to_all(
        outputs.reshape(experts, items, width), "expert", split_axis=0, concat_axis=0, tiled=True
    )
    gate_three = gate_pre.reshape(experts, items, inner)
    up_three = up_pre.reshape(experts, items, inner)
    hidden_three = hidden.reshape(experts, items, inner)
    inputs = block.reshape(-1, width)
    gate_pre = gate_three.reshape(-1, inner)
    up_pre = up_three.reshape(-1, inner)
    hidden = hidden_three.reshape(-1, inner)
    gathered = back_items.reshape(-1, width)[slots].reshape(rows_dev, picks, width)
    mixed = jnp.sum(gates[:, :, None] * gathered.astype(jnp.float32), axis=1).astype(jnp.bfloat16)
    cot_pad = jnp.concatenate([cotangent, jnp.zeros((1, width), cotangent.dtype)], axis=0)
    cot_send = (weight_of[:, None] * cot_pad[token_of].astype(jnp.float32)).astype(jnp.bfloat16)
    slot_cot = lax.all_to_all(
        cot_send.reshape(experts, capacity, width),
        "expert",
        split_axis=0,
        concat_axis=0,
        tiled=True,
    ).reshape(-1, width)
    down_part = jnp.dot(hidden.T, slot_cot, preferred_element_type=jnp.float32)
    hidden_grad = jnp.dot(slot_cot, down_mat.T, preferred_element_type=jnp.float32)
    sigma = jax.nn.sigmoid(gate_pre)
    gate_grad = (hidden_grad * up_pre * sigma * (1.0 + gate_pre * (1.0 - sigma))).astype(
        jnp.bfloat16
    )
    up_grad = (hidden_grad * gate_pre * sigma).astype(jnp.bfloat16)
    slot_grads = (
        jnp.dot(gate_grad, gate_mat.T, preferred_element_type=jnp.float32)
        + jnp.dot(up_grad, up_mat.T, preferred_element_type=jnp.float32)
    ).astype(jnp.bfloat16)
    grads_back = lax.all_to_all(
        slot_grads.reshape(experts, capacity, width),
        "expert",
        split_axis=0,
        concat_axis=0,
        tiled=True,
    )
    gate_part = jnp.dot(inputs.T, gate_grad, preferred_element_type=jnp.float32)
    up_part = jnp.dot(inputs.T, up_grad, preferred_element_type=jnp.float32)
    gate_total, up_total, down_total = (
        lax.psum(gate_part.astype(jnp.bfloat16), "pipe").astype(jnp.float32),
        lax.psum(up_part.astype(jnp.bfloat16), "pipe").astype(jnp.float32),
        lax.psum(down_part.astype(jnp.bfloat16), "pipe").astype(jnp.float32),
    )
    grad_rows = grads_back.reshape(-1, width)[slots].reshape(rows_dev, picks, width)
    input_grad = jnp.sum(grad_rows.astype(jnp.float32), axis=1).astype(jnp.bfloat16)
    return (
        mixed,
        input_grad,
        gate_total.astype(jnp.bfloat16)[None],
        up_total.astype(jnp.bfloat16)[None],
        down_total.astype(jnp.bfloat16)[None],
    )


def solution(mesh):
    in_specs = (
        P(("pipe", "expert"), None),
        P(("pipe", "expert"), None),
        P(("pipe", "expert"), None),
        P(("pipe", "expert"), None),
        P("expert", None, None),
        P("expert", None, None),
        P("expert", None, None),
    )
    out_specs = (
        P(("pipe", "expert"), None),
        P(("pipe", "expert"), None),
        P("expert", None, None),
        P("expert", None, None),
        P("expert", None, None),
    )
    return jax.shard_map(
        on_device, mesh=mesh, in_specs=in_specs, out_specs=out_specs, check_vma=False
    )
```

profile of v0, /device:TPU:14, one launch (start us, length us, event | category | flops | bytes accessed | tf_op | source)
XLA Modules:
  0.0 467.3 jit_solution(10504910093243393587)
XLA Ops:
  7.2 0.8 broadcast_multiply_fusion
  9.2 4.5 reduce-window.6
  14.2 4.3 scatter_custom_fusion
  18.5 1.1 concatenate.6
  19.6 6.1 %gather_fusion = bf16[1024,2048]{1,0:T(8,128)(2,1)} fusion(bf16[129,2048]{1,0:T(8,128)(2,1)S(1)} %concatenate.6, s32[1024]{0:T(1024)S(1)} %fusion.21), kind=kCustom, calls=%fused_computation | custom fusion | bytes 8392704 | tf_op jit(solution)/shard_map/gather | solution.py:39
  25.7 7.3 %all-to-all-start = ((bf16[16,64,2048]{2,1,0:T(8,128)(2,1)}), bf16[16,64,2048]{2,1,0:T(8,128)(2,1)}, u32[]{:S(2)}, u32[]{:S(2)}) async-start(bf16[16,64,2048]{2,1,0:T(8,128)(2,1)} %bitcast.73), calls=%async_computation | async-start | bytes 8388608 | tf_op jit(solution)/shard_map/all_to_all | solution.py:40
  33.1 4.3 scatter_custom_fusion.1
  37.6 6.0 %gather_fusion.2 = bf16[1024,2048]{1,0:T(8,128)(2,1)} fusion(bf16[129,2048]{1,0:T(8,128)(2,1)S(1)} %concatenate.7, s32[1024]{0:T(1024)S(1)} %fusion.21), kind=kCustom, calls=%fused_computation.2 | custom fusion | bytes 8392704 | tf_op jit(solution)/shard_map/gather | solution.py:56
  43.6 4.9 %fusion = bf16[16,64,2048]{2,1,0:T(8,128)(2,1)} fusion(bf16[16,64,2048]{2,1,0:T(8,128)(2,1)} %bitcast.71, f32[16,64]{1,0:T(8,128)S(1)} %mul.70), kind=kLoop, calls=%fused_computation.7 | loop fusion | flops 6291456 | bytes 8392704 | tf_op jit(solution)/shard_map/convert_element_type | solution.py:56
  48.5 79.1 %all-to-all-done = bf16[16,64,2048]{2,1,0:T(8,128)(2,1)} async-done(((bf16[16,64,2048]{2,1,0:T(8,128)(2,1)}), bf16[16,64,2048]{2,1,0:T(8,128)(2,1)}, u32[]{:S(2)}, u32[]{:S(2)}) %all-to-all-start) | async-done | bytes 4194336 | tf_op jit(solution)/shard_map/all_to_all | solution.py:40
  127.6 5.1 %all-to-all-start.2 = ((bf16[16,64,2048]{2,1,0:T(8,128)(2,1)}), bf16[16,64,2048]{2,1,0:T(8,128)(2,1)}, u32[]{:S(2)}, u32[]{:S(2)}) async-start(bf16[16,64,2048]{2,1,0:T(8,128)(2,1)} %fusion), calls=%async_computation.2 | async-start | bytes 8388608 | tf_op jit(solution)/shard_map/all_to_all | solution.py:57
  132.7 6.2 %fusion.9 = f32[1024,384]{1,0:T(8,128)} fusion(bf16[1024,2048]{1,0:T(8,128)(2,1)} %bitcast.5, bf16[1,2048,384]{2,1,0:T(8,128)(2,1)} %param.12), kind=kOutput, calls=%fused_computation.23 | convolution fusion | flops 1610612736 | bytes 7340032 | tf_op jit(solution)/shard_map/dot_general | solution.py:18
  139.0 5.7 %fusion.13 = f32[1024,384]{1,0:T(8,128)} fusion(bf16[1024,2048]{1,0:T(8,128)(2,1)} %bitcast.5, bf16[1,2048,384]{2,1,0:T(8,128)(2,1)S(1)} %copy-done.3), kind=kOutput, calls=%fused_computation.27 | convolution fusion | flops 1610612736 | bytes 7340032 | tf_op jit(solution)/shard_map/dot_general | solution.py:17
  144.6 80.7 %all-to-all-done.2 = bf16[16,64,2048]{2,1,0:T(8,128)(2,1)} async-done(((bf16[16,64,2048]{2,1,0:T(8,128)(2,1)}), bf16[16,64,2048]{2,1,0:T(8,128)(2,1)}, u32[]{:S(2)}, u32[]{:S(2)}) %all-to-all-start.2) | async-done | bytes 4194336 | tf_op jit(solution)/shard_map/all_to_all | solution.py:57
  225.4 7.2 %multiply_convert_fusion = (bf16[1024,384]{1,0:T(8,128)(2,1)}, bf16[1024,384]{1,0:T(8,128)(2,1)}, bf16[1024,384]{1,0:T(8,128)(2,1)S(1)}) fusion(f32[1024,384]{1,0:T(8,128)} %fusion.13, f32[1024,384]{1,0:T(8,128)} %fusion.9, bf16[1024,2048]{1,0:T(8,128)(2,1)} %bitcast.13, bf16[1,384,2048]{2,1,0:T(8,128)(2,1)S(1)} %copy-done), kind=kOutput, calls=%fused_computation.29 | convolution fusion | flops 1616904192 | bytes 11272192 | tf_op jit(solution)/shard_map/dot_general | solution.py:65
  232.6 4.3 convolution_convert_fusion
  236.9 5.1 %all-to-all-start.1 = ((bf16[16,64,2048]{2,1,0:T(8,128)(2,1)}), bf16[16,64,2048]{2,1,0:T(8,128)(2,1)}, u32[]{:S(2)}, u32[]{:S(2)}) async-start(bf16[16,64,2048]{2,1,0:T(8,128)(2,1)} %bitcast.74), calls=%async_computation.1 | async-start | bytes 8388608 | tf_op jit(solution)/shard_map/all_to_all | solution.py:43
  242.0 3.6 fusion.11
  245.7 4.3 add_convert_fusion
  250.0 84.6 %all-to-all-done.1 = bf16[16,64,2048]{2,1,0:T(8,128)(2,1)} async-done(((bf16[16,64,2048]{2,1,0:T(8,128)(2,1)}), bf16[16,64,2048]{2,1,0:T(8,128)(2,1)}, u32[]{:S(2)}, u32[]{:S(2)}) %all-to-all-start.1) | async-done | bytes 4194336 | tf_op jit(solution)/shard_map/all_to_all | solution.py:43
  334.6 5.2 %all-to-all-start.3 = ((bf16[16,64,2048]{2,1,0:T(8,128)(2,1)}), bf16[16,64,2048]{2,1,0:T(8,128)(2,1)}, u32[]{:S(2)}, u32[]{:S(2)}) async-start(bf16[16,64,2048]{2,1,0:T(8,128)(2,1)} %bitcast.72), calls=%async_computation.3 | async-start | bytes 8388608 | tf_op jit(solution)/shard_map/all_to_all | solution.py:75
  339.9 5.2 %fusion.4 = bf16[1,384,2048]{2,1,0:T(8,128)(2,1)} fusion(bf16[1024,384]{1,0:T(8,128)(2,1)S(1)} %copy-done.13, bf16[1024,2048]{1,0:T(8,128)(2,1)} %bitcast.13), kind=kOutput, calls=%fused_computation.18 | convolution fusion | flops 1611399168 | bytes 6553600 | tf_op jit(solution)/shard_map/dot_general | solution.py:64
  345.2 5.8 %fusion.3 = bf16[1,2048,384]{2,1,0:T(8,128)(2,1)} fusion(bf16[1024,2048]{1,0:T(8,128)(2,1)} %bitcast.5, bf16[1024,384]{1,0:T(8,128)(2,1)S(1)} %copy-done.9), kind=kOutput, calls=%fused_computation.17 | convolution fusion | flops 1611399168 | bytes 6553600 | tf_op jit(solution)/shard_map/dot_general | solution.py:83
  351.0 5.7 %fusion.2 = bf16[1,2048,384]{2,1,0:T(8,128)(2,1)} fusion(bf16[1024,2048]{1,0:T(8,128)(2,1)} %bitcast.5, bf16[1024,384]{1,0:T(8,128)(2,1)S(1)} %copy-done.7), kind=kOutput, calls=%fused_computation.16 | convolution fusion | flops 1611399168 | bytes 6553600 | tf_op jit(solution)/shard_map/dot_general | solution.py:82
  356.7 11.8 %gather_fusion.1 = bf16[1024,2048]{1,0:T(8,128)(2,1)} fusion(bf16[1024,2048]{1,0:T(8,128)(2,1)} %bitcast.10, s32[1024]{0:T(1024)S(1)} %broadcast_clamp_fusion), kind=kCustom, calls=%fused_computation.1 | custom fusion | bytes 8392704 | tf_op jit(solution)/shard_map/gather | solution.py:53
  368.5 64.0 %all-to-all-done.3 = bf16[16,64,2048]{2,1,0:T(8,128)(2,1)} async-done(((bf16[16,64,2048]{2,1,0:T(8,128)(2,1)}), bf16[16,64,2048]{2,1,0:T(8,128)(2,1)}, u32[]{:S(2)}, u32[]{:S(2)}) %all-to-all-start.3) | async-done | bytes 4194336 | tf_op jit(solution)/shard_map/all_to_all | solution.py:75
  432.5 11.6 %gather_fusion.3 = bf16[1024,2048]{1,0:T(8,128)(2,1)} fusion(bf16[1024,2048]{1,0:T(8,128)(2,1)} %bitcast.15, s32[1024]{0:T(1024)S(1)} %broadcast_clamp_fusion), kind=kCustom, calls=%fused_computation.3 | custom fusion | bytes 8392704 | tf_op jit(solution)/shard_map/gather | solution.py:89
  444.1 6.0 %bitcast_reduce_fusion = bf16[128,2048]{1,0:T(8,128)(2,1)} fusion(bf16[1024,2048]{1,0:T(8,128)(2,1)} %gather_fusion.3), kind=kLoop, calls=%fused_computation.11 | loop fusion | flops 1835008 | bytes 4718592 | tf_op jit(solution)/shard_map/reduce_sum | solution.py:90
  450.1 5.2 %fusion.1 = bf16[128,2048]{1,0:T(8,128)(2,1)} fusion(bf16[1024,2048]{1,0:T(8,128)(2,1)S(1)} %copy-done.2, f32[128,8]{1,0:T(8,128)S(1)} %copy.15), kind=kLoop, calls=%fused_computation.9 | loop fusion | flops 6029312 | bytes 4722688 | tf_op jit(solution)/shard_map/reduce_sum | solution.py:54
  455.3 2.9 copy.27
  458.2 1.1 copy.28
  459.3 1.1 copy.29
  (52 shorter events, 2.1 us)
Async XLA Ops:
  7.2 218.2 %copy-start = (bf16[1,384,2048]{2,1,0:T(8,128)(2,1)S(1)}, bf16[1,384,2048]{2,1,0:T(8,128)(2,1)}, u32[]{:S(2)}) copy-start(bf16[1,384,2048]{2,1,0:T(8,128)(2,1)} %param.13) | copy-start | bytes 4718596
  25.7 7.3 %copy-start.11 = (f32[128,8]{0,1:T(8,128)S(1)}, f32[128,8]{0,1:T(8,128)}, u32[]{:S(2)}) copy-start(f32[128,8]{0,1:T(8,128)} %param.9) | copy-start | bytes 12292
  25.7 11.9 %copy-start.10 = (bf16[128,2048]{1,0:T(8,128)(2,1)S(1)}, bf16[128,2048]{1,0:T(8,128)(2,1)}, u32[]{:S(2)}) copy-start(bf16[128,2048]{1,0:T(8,128)(2,1)} %param.10) | copy-start | bytes 1572868
  25.7 101.9 %all-to-all-start = ((bf16[16,64,2048]{2,1,0:T(8,128)(2,1)}), bf16[16,64,2048]{2,1,0:T(8,128)(2,1)}, u32[]{:S(2)}, u32[]{:S(2)}) async-start(bf16[16,64,2048]{2,1,0:T(8,128)(2,1)} %bitcast.73), calls=%async_computation | async-start | bytes 8388608 | tf_op jit(solution)/shard_map/all_to_all | solution.py:40
  127.6 97.8 %all-to-all-start.2 = ((bf16[16,64,2048]{2,1,0:T(8,128)(2,1)}), bf16[16,64,2048]{2,1,0:T(8,128)(2,1)}, u32[]{:S(2)}, u32[]{:S(2)}) async-start(bf16[16,64,2048]{2,1,0:T(8,128)(2,1)} %fusion), calls=%async_computation.2 | async-start | bytes 8388608 | tf_op jit(solution)/shard_map/all_to_all | solution.py:57
  132.7 6.3 %copy-start.3 = (bf16[1,2048,384]{2,1,0:T(8,128)(2,1)S(1)}, bf16[1,2048,384]{2,1,0:T(8,128)(2,1)}, u32[]{:S(2)}) copy-start(bf16[1,2048,384]{2,1,0:T(8,128)(2,1)} %param.11) | copy-start | bytes 4718596
  232.6 4.3 copy-start.12
  236.9 97.8 %all-to-all-start.1 = ((bf16[16,64,2048]{2,1,0:T(8,128)(2,1)}), bf16[16,64,2048]{2,1,0:T(8,128)(2,1)}, u32[]{:S(2)}, u32[]{:S(2)}) async-start(bf16[16,64,2048]{2,1,0:T(8,128)(2,1)} %bitcast.74), calls=%async_computation.1 | async-start | bytes 8388608 | tf_op jit(solution)/shard_map/all_to_all | solution.py:43
  242.0 3.7 copy-start.4
  242.0 3.7 copy-start.8
  334.6 5.3 %copy-start.13 = (bf16[1024,384]{1,0:T(8,128)(2,1)S(1)}, bf16[1024,384]{1,0:T(8,128)(2,1)}, u32[]{:S(2)}) copy-start(bf16[1024,384]{1,0:T(8,128)(2,1)} %copy-done.12) | copy-start | bytes 2359300
  334.6 97.9 %all-to-all-start.3 = ((bf16[16,64,2048]{2,1,0:T(8,128)(2,1)}), bf16[16,64,2048]{2,1,0:T(8,128)(2,1)}, u32[]{:S(2)}, u32[]{:S(2)}) async-start(bf16[16,64,2048]{2,1,0:T(8,128)(2,1)} %bitcast.72), calls=%async_computation.3 | async-start | bytes 8388608 | tf_op jit(solution)/shard_map/all_to_all | solution.py:75
  339.9 5.3 %copy-start.9 = (bf16[1024,384]{1,0:T(8,128)(2,1)S(1)}, bf16[1024,384]{1,0:T(8,128)(2,1)}, u32[]{:S(2)}) copy-start(bf16[1024,384]{1,0:T(8,128)(2,1)} %get-tuple-element.8) | copy-start | bytes 2359300
  339.9 115.4 %all-reduce.5.cloned.1.call-start = ((), (), s32[]{:S(2)}) async-start(), calls=%async_computation.4 | async-start | bytes 9437184 | tf_op jit(solution)/shard_map/psum | solution.py:85
  345.2 5.8 %copy-start.7 = (bf16[1024,384]{1,0:T(8,128)(2,1)S(1)}, bf16[1024,384]{1,0:T(8,128)(2,1)}, u32[]{:S(2)}) copy-start(bf16[1024,384]{1,0:T(8,128)(2,1)} %get-tuple-element.9) | copy-start | bytes 2359300
  444.1 6.0 %copy-start.2 = (bf16[1024,2048]{1,0:T(8,128)(2,1)S(1)}, bf16[1024,2048]{1,0:T(8,128)(2,1)}, u32[]{:S(2)}) copy-start(bf16[1024,2048]{1,0:T(8,128)(2,1)} %gather_fusion.1) | copy-start | bytes 12582916
  455.3 2.9 copy-start.6
  455.3 4.0 copy-start.5
  455.3 5.2 %copy-start.1 = (bf16[1,384,2048]{2,1,0:T(8,128)(2,1)S(1)}, bf16[1,384,2048]{2,1,0:T(8,128)(2,1)}, u32[]{:S(2)}) copy-start(bf16[1,384,2048]{2,1,0:T(8,128)(2,1)} %param.13) | copy-start | bytes 4718596
Sparse Core Ops, SparseCore 0:
  356.8 30.5 all-reduce.4
where the time goes:
time: 468 us; the launch traced here: 467 us
  waiting for transfers between devices  309 us (66%)
  local copies, waits for them, and re-layouts  52.1 us (11%)
  matrix products  48.1 us (10%)
  starting transfers between devices  22.8 us (5%)
  other arithmetic  21.6 us (5%)
  between operations  14.2 us (3%)
    all_to_all x1, waiting for transfers between devices, on_device(): lax.all_to_all(outputs.reshape(experts, items, width), 'expert', split_ax...  84.6 us
    all_to_all x1, waiting for transfers between devices, on_device(): lax.all_to_all(cot_send.reshape(experts, capacity, width), 'expert', spli...  80.7 us
    all_to_all x1, waiting for transfers between devices, on_device(): lax.all_to_all(send, 'expert', split_axis=0, concat_axis=0, tiled=True)  79.1 us
    all_to_all x1, waiting for transfers between devices, on_device(): lax.all_to_all(slot_grads.reshape(experts, capacity, width), 'expert', sp...  64 us
    gather x1, local copies, waits for them, and re-layouts, on_device(): back_items.reshape(-1, width)[slots].reshape(rows_dev, picks, width)  11.8 us
    gather x1, local copies, waits for them, and re-layouts, on_device(): grads_back.reshape(-1, width)[slots].reshape(rows_dev, picks, width)  11.6 us
  transfers between devices with their start and end apart: 5, of which 4 were waited for; matrix products, arithmetic and copies ran while one was open for 19% of the time, Pallas kernels for 0%

commit v1 on v0

--- a/solution.py
+++ b/solution.py
@@ -1,7 +1,38 @@
+import functools
 import jax
 import jax.numpy as jnp
 from jax import lax
 from jax.sharding import PartitionSpec as P
+
+
+def name_chunk_in(u, in_dim, mine):
+    upper, y_new = (u.shape[:in_dim], u.shape[in_dim + 1 :])
+    z1 = jnp.moveaxis(u.reshape(*upper, mine, -1, *y_new), in_dim, 0)
+    return z1
+
+
+def _fill_loops(array_in, axis_no):
+    outcome_arr = list(array_in.shape[1:])
+    outcome_arr[axis_no] *= array_in.shape[0]
+    known = jnp.moveaxis(array_in, 0, axis_no).reshape(outcome_arr)
+    return known
+
+
+def update_the_lots_all(original, net_axis, local_x, message):
+    w2, base_arr = (lax.axis_size(net_axis), lax.axis_index(net_axis))
+    local_part = name_chunk_in(original, local_x, w2)
+    blocks_here = [local_part[base_arr]]
+    p = 1
+    while p < w2:
+        found_now = local_part[base_arr ^ p]
+        blocks_here.append(lax.ppermute(found_now, net_axis, [(nth, nth ^ p) for nth in range(w2)]))
+        p += 1
+    local_part = jnp.stack(blocks_here, axis=0)[base_arr ^ jnp.arange(w2)]
+    row_out = _fill_loops(local_part, message)
+    return row_out
+
+
+start_the_slot = functools.partial(update_the_lots_all, net_axis="expert", local_x=0, message=0)
 
 
 def slot_index(block_routes, expert_count, capacity):
@@ -40,9 +71,7 @@
     block = lax.all_to_all(send, "expert", split_axis=0, concat_axis=0, tiled=True)
     items = block.shape[1]
     gate_pre, up_pre, hidden, outputs = expert_forward(block, gate_mat, up_mat, down_mat)
-    back_items = lax.all_to_all(
-        outputs.reshape(experts, items, width), "expert", split_axis=0, concat_axis=0, tiled=True
-    )
+    back_items = start_the_slot(outputs.reshape(experts, items, width))
     gate_three = gate_pre.reshape(experts, items, inner)
     up_three = up_pre.reshape(experts, items, inner)
     hidden_three = hidden.reshape(experts, items, inner)

time: 468 us -> 527 us (1.13)
  the two profiles are of different devices: /device:TPU:14 before, /device:TPU:4 now
where the time goes in v1:
time: 527 us; the launch traced here: 526 us
  waiting for transfers between devices  311 us (59%)
  local copies, waits for them, and re-layouts  76.4 us (14%)
  starting transfers between devices  55 us (10%)
  matrix products  46 us (9%)
  other arithmetic  23.6 us (4%)
  between operations  14.2 us (3%)
    ppermute x15, waiting for transfers between devices, update_the_lots_all(): lax.ppermute(found_now, net_axis, [(nth, nth ^ p) for nth in range(w2)])  171 us
    all_to_all x1, waiting for transfers between devices, on_device(): lax.all_to_all(cot_send.reshape(experts, capacity, width), 'expert', spli...  70.9 us
    all_to_all x1, waiting for transfers between devices, on_device(): lax.all_to_all(send, 'expert', split_axis=0, concat_axis=0, tiled=True)  69.3 us
    unnamed x39, local copies, waits for them, and re-layouts  20.1 us
    ppermute x15, starting transfers between devices, update_the_lots_all(): lax.ppermute(found_now, net_axis, [(nth, nth ^ p) for nth in range(w2)])  17.7 us
    all_to_all x1, starting transfers between devices, on_device(): lax.all_to_all(slot_grads.reshape(experts, capacity, width), 'expert', sp...  14.9 us
    all_to_all x1, starting transfers between devices, on_device(): lax.all_to_all(cot_send.reshape(experts, capacity, width), 'expert', spli...  14.9 us
    gather x1, local copies, waits for them, and re-layouts, on_device(): back_items.reshape(-1, width)[slots].reshape(rows_dev, picks, width)  11.8 us
  transfers between devices with their start and end apart: 19, of which 13 were waited for; matrix products, arithmetic and copies ran while one was open for 18% of the time, Pallas kernels for 0%

profile of v1, /device:TPU:4, one launch (start us, length us, event | category | flops | bytes accessed | tf_op | source)
XLA Modules:
  0.0 526.0 jit_solution(8492351457403559349)
XLA Ops:
  9.2 4.5 reduce-window.6
  19.6 6.1 %gather_fusion = bf16[1024,2048]{1,0:T(8,128)(2,1)} fusion(bf16[129,2048]{1,0:T(8,128)(2,1)S(1)} %concatenate.6, s32[1024]{0:T(1024)S(1)} %fusion.21), kind=kCustom, calls=%fused_computation | custom fusion | bytes 8392704 | tf_op jit(solution)/shard_map/gather | solution.py:70
  25.7 7.4 %all-to-all-start = ((bf16[16,64,2048]{2,1,0:T(8,128)(2,1)}), bf16[16,64,2048]{2,1,0:T(8,128)(2,1)}, u32[]{:S(2)}, u32[]{:S(2)}) async-start(bf16[16,64,2048]{2,1,0:T(8,128)(2,1)} %bitcast.137), calls=%async_computation | async-start | bytes 8388608 | tf_op jit(solution)/shard_map/all_to_all | solution.py:71
  37.7 6.1 %gather_fusion.3 = bf16[1024,2048]{1,0:T(8,128)(2,1)} fusion(bf16[129,2048]{1,0:T(8,128)(2,1)S(1)} %concatenate.7, s32[1024]{0:T(1024)S(1)} %fusion.21), kind=kCustom, calls=%fused_computation.3 | custom fusion | bytes 8392704 | tf_op jit(solution)/shard_map/gather | solution.py:85
  43.8 4.9 fusion
  48.7 69.3 %all-to-all-done = bf16[16,64,2048]{2,1,0:T(8,128)(2,1)} async-done(((bf16[16,64,2048]{2,1,0:T(8,128)(2,1)}), bf16[16,64,2048]{2,1,0:T(8,128)(2,1)}, u32[]{:S(2)}, u32[]{:S(2)}) %all-to-all-start) | async-done | bytes 4194336 | tf_op jit(solution)/shard_map/all_to_all | solution.py:71
  118.0 14.9 %all-to-all-start.1 = ((bf16[16,64,2048]{2,1,0:T(8,128)(2,1)}), bf16[16,64,2048]{2,1,0:T(8,128)(2,1)}, u32[]{:S(2)}, u32[]{:S(2)}) async-start(bf16[16,64,2048]{2,1,0:T(8,128)(2,1)} %fusion), calls=%async_computation.1 | async-start | bytes 8388608 | tf_op jit(solution)/shard_map/all_to_all | solution.py:86
  132.9 6.3 %fusion.9 = f32[1024,384]{1,0:T(8,128)} fusion(bf16[1024,2048]{1,0:T(8,128)(2,1)} %bitcast.5, bf16[1,2048,384]{2,1,0:T(8,128)(2,1)} %param.12), kind=kOutput, calls=%fused_computation.24 | convolution fusion | flops 1610612736 | bytes 7340032 | tf_op jit(solution)/shard_map/dot_general | solution.py:49
  139.2 5.7 %fusion.13 = f32[1024,384]{1,0:T(8,128)} fusion(bf16[1024,2048]{1,0:T(8,128)(2,1)} %bitcast.5, bf16[1,2048,384]{2,1,0:T(8,128)(2,1)S(1)} %copy-done.2), kind=kOutput, calls=%fused_computation.28 | convolution fusion | flops 1610612736 | bytes 7340032 | tf_op jit(solution)/shard_map/dot_general | solution.py:48
  144.8 70.9 %all-to-all-done.1 = bf16[16,64,2048]{2,1,0:T(8,128)(2,1)} async-done(((bf16[16,64,2048]{2,1,0:T(8,128)(2,1)}), bf16[16,64,2048]{2,1,0:T(8,128)(2,1)}, u32[]{:S(2)}, u32[]{:S(2)}) %all-to-all-start.1) | async-done | bytes 4194336 | tf_op jit(solution)/shard_map/all_to_all | solution.py:86
  215.7 6.0 %multiply_convert_fusion = (bf16[1024,384]{1,0:T(8,128)(2,1)S(1)}, bf16[1024,384]{1,0:T(8,128)(2,1)S(1)}, bf16[1024,384]{1,0:T(8,128)(2,1)S(1)}) fusion(f32[1024,384]{1,0:T(8,128)} %fusion.13, f32[1024,384]{1,0:T(8,128)} %fusion.9, bf16[1024,2048]{1,0:T(8,128)(2,1)} %bitcast.45, bf16[1,384,2048]{2,1,0:T(8,128)(2,1)S(1)} %copy-done), kind=kOutput, calls=%fused_computation.30 | convolution fusion | flops 1616904192 | bytes 11272192 | tf_op jit(solution)/shard_map/dot_general | solution.py:94
  221.7 6.0 %fusion.2 = bf16[1,2048,384]{2,1,0:T(8,128)(2,1)} fusion(bf16[1024,2048]{1,0:T(8,128)(2,1)} %bitcast.5, bf16[1024,384]{1,0:T(8,128)(2,1)S(1)} %get-tuple-element.25), kind=kOutput, calls=%fused_computation.17 | convolution fusion | flops 1611399168 | bytes 6553600 | tf_op jit(solution)/shard_map/dot_general | solution.py:111
  230.1 5.7 %fusion.3 = bf16[1,2048,384]{2,1,0:T(8,128)(2,1)} fusion(bf16[1024,2048]{1,0:T(8,128)(2,1)} %bitcast.5, bf16[1024,384]{1,0:T(8,128)(2,1)S(1)} %get-tuple-element.24), kind=kOutput, calls=%fused_computation.18 | convolution fusion | flops 1611399168 | bytes 6553600 | tf_op jit(solution)/shard_map/dot_general | solution.py:112
  235.8 4.5 convolution_convert_fusion
  244.7 14.9 %all-to-all-start.2 = ((bf16[16,64,2048]{2,1,0:T(8,128)(2,1)}), bf16[16,64,2048]{2,1,0:T(8,128)(2,1)}, u32[]{:S(2)}, u32[]{:S(2)}) async-start(bf16[16,64,2048]{2,1,0:T(8,128)(2,1)} %bitcast.136), calls=%async_computation.2 | async-start | bytes 8388608 | tf_op jit(solution)/shard_map/all_to_all | solution.py:104
  274.1 5.2 fusion.4
  281.6 9.1 %collective-permute-done.1 = bf16[1,64,2048]{2,1,0:T(8,128)(2,1)S(1)} collective-permute-done((bf16[1,64,2048]{2,1,0:T(8,128)(2,1)}, bf16[1,64,2048]{2,1,0:T(8,128)(2,1)S(1)}, u32[]{:S(2)}, u32[]{:S(2)}) %collective-permute-start.1) | collective-permute-done | bytes 262176 | tf_op jit(solution)/shard_map/ppermute | solution.py:28
  292.0 29.5 %collective-permute-done.2 = bf16[1,64,2048]{2,1,0:T(8,128)(2,1)S(1)} collective-permute-done((bf16[1,64,2048]{2,1,0:T(8,128)(2,1)S(1)}, bf16[1,64,2048]{2,1,0:T(8,128)(2,1)S(1)}, u32[]{:S(2)}, u32[]{:S(2)}) %collective-permute-start.2) | collective-permute-done | bytes 262176 | tf_op jit(solution)/shard_map/ppermute | solution.py:28
  322.3 47.0 %collective-permute-done.3 = bf16[1,64,2048]{2,1,0:T(8,128)(2,1)S(1)} collective-permute-done((bf16[1,64,2048]{2,1,0:T(8,128)(2,1)S(1)}, bf16[1,64,2048]{2,1,0:T(8,128)(2,1)S(1)}, u32[]{:S(2)}, u32[]{:S(2)}) %collective-permute-start.3) | collective-permute-done | bytes 262176 | tf_op jit(solution)/shard_map/ppermute | solution.py:28
  370.0 7.2 %collective-permute-done.4 = bf16[1,64,2048]{2,1,0:T(8,128)(2,1)S(1)} collective-permute-done((bf16[1,64,2048]{2,1,0:T(8,128)(2,1)S(1)}, bf16[1,64,2048]{2,1,0:T(8,128)(2,1)S(1)}, u32[]{:S(2)}, u32[]{:S(2)}) %collective-permute-start.4) | collective-permute-done | bytes 262176 | tf_op jit(solution)/shard_map/ppermute | solution.py:28
  377.9 9.7 %collective-permute-done.5 = bf16[1,64,2048]{2,1,0:T(8,128)(2,1)S(1)} collective-permute-done((bf16[1,64,2048]{2,1,0:T(8,128)(2,1)S(1)}, bf16[1,64,2048]{2,1,0:T(8,128)(2,1)S(1)}, u32[]{:S(2)}, u32[]{:S(2)}) %collective-permute-start.5) | collective-permute-done | bytes 262176 | tf_op jit(solution)/shard_map/ppermute | solution.py:28
  388.4 7.4 %collective-permute-done.6 = bf16[1,64,2048]{2,1,0:T(8,128)(2,1)S(1)} collective-permute-done((bf16[1,64,2048]{2,1,0:T(8,128)(2,1)S(1)}, bf16[1,64,2048]{2,1,0:T(8,128)(2,1)S(1)}, u32[]{:S(2)}, u32[]{:S(2)}) %collective-permute-start.6) | collective-permute-done | bytes 262176 | tf_op jit(solution)/shard_map/ppermute | solution.py:28
  395.8 5.0 collective-permute-start.7
  401.5 32.0 %collective-permute-done.7 = bf16[1,64,2048]{2,1,0:T(8,128)(2,1)S(1)} collective-permute-done((bf16[1,64,2048]{2,1,0:T(8,128)(2,1)S(1)}, bf16[1,64,2048]{2,1,0:T(8,128)(2,1)S(1)}, u32[]{:S(2)}, u32[]{:S(2)}) %collective-permute-start.7) | collective-permute-done | bytes 262176 | tf_op jit(solution)/shard_map/ppermute | solution.py:28
  434.2 10.7 %collective-permute-done.8 = bf16[1,64,2048]{2,1,0:T(8,128)(2,1)S(1)} collective-permute-done((bf16[1,64,2048]{2,1,0:T(8,128)(2,1)S(1)}, bf16[1,64,2048]{2,1,0:T(8,128)(2,1)S(1)}, u32[]{:S(2)}, u32[]{:S(2)}) %collective-permute-start.8) | collective-permute-done | bytes 262176 | tf_op jit(solution)/shard_map/ppermute | solution.py:28
  445.7 9.3 %collective-permute-done.9 = bf16[1,64,2048]{2,1,0:T(8,128)(2,1)S(1)} collective-permute-done((bf16[1,64,2048]{2,1,0:T(8,128)(2,1)S(1)}, bf16[1,64,2048]{2,1,0:T(8,128)(2,1)S(1)}, u32[]{:S(2)}, u32[]{:S(2)}) %collective-permute-start.9) | collective-permute-done | bytes 262176 | tf_op jit(solution)/shard_map/ppermute | solution.py:28
  456.7 8.4 %collective-permute-done.10 = bf16[1,64,2048]{2,1,0:T(8,128)(2,1)S(1)} collective-permute-done((bf16[1,64,2048]{2,1,0:T(8,128)(2,1)S(1)}, bf16[1,64,2048]{2,1,0:T(8,128)(2,1)S(1)}, u32[]{:S(2)}, u32[]{:S(2)}) %collective-permute-start.10) | collective-permute-done | bytes 262176 | tf_op jit(solution)/shard_map/ppermute | solution.py:28
  472.5 5.0 gather_fusion.1
  477.4 11.8 %gather_fusion.2 = bf16[1024,2048]{1,0:T(8,128)(2,1)} fusion(bf16[1024,2048]{1,0:T(8,128)(2,1)} %bitcast.134, s32[1024]{0:T(1024)S(1)} %broadcast_clamp_fusion), kind=kCustom, calls=%fused_computation.2 | custom fusion | bytes 8392704 | tf_op jit(solution)/shard_map/gather | solution.py:82
  489.2 7.3 %fusion.1 = bf16[128,2048]{1,0:T(8,128)(2,1)} fusion(bf16[1024,2048]{1,0:T(8,128)(2,1)} %gather_fusion.2, f32[128,8]{1,0:T(8,128)S(1)} %copy.15), kind=kLoop, calls=%fused_computation.10 | loop fusion | flops 6029312 | bytes 4722688 | tf_op jit(solution)/shard_map/reduce_sum | solution.py:83
  496.6 11.6 %gather_fusion.4 = bf16[1024,2048]{1,0:T(8,128)(2,1)} fusion(bf16[1024,2048]{1,0:T(8,128)(2,1)} %bitcast.47, s32[1024]{0:T(1024)S(1)} %broadcast_clamp_fusion), kind=kCustom, calls=%fused_computation.4 | custom fusion | bytes 8392704 | tf_op jit(solution)/shard_map/gather | solution.py:118
  508.2 5.9 %bitcast_reduce_fusion = bf16[128,2048]{1,0:T(8,128)(2,1)} fusion(bf16[1024,2048]{1,0:T(8,128)(2,1)} %gather_fusion.4), kind=kLoop, calls=%fused_computation.12 | loop fusion | flops 1835008 | bytes 4718592 | tf_op jit(solution)/shard_map/reduce_sum | solution.py:119
  (91 shorter events, 56.7 us)
Async XLA Ops:
  7.2 208.6 %copy-start = (bf16[1,384,2048]{2,1,0:T(8,128)(2,1)S(1)}, bf16[1,384,2048]{2,1,0:T(8,128)(2,1)}, u32[]{:S(2)}) copy-start(bf16[1,384,2048]{2,1,0:T(8,128)(2,1)} %param.13) | copy-start | bytes 4718596
  25.7 7.4 %copy-start.7 = (f32[128,8]{0,1:T(8,128)S(1)}, f32[128,8]{0,1:T(8,128)}, u32[]{:S(2)}) copy-start(f32[128,8]{0,1:T(8,128)} %param.9) | copy-start | bytes 12292
  25.7 12.0 %copy-start.6 = (bf16[128,2048]{1,0:T(8,128)(2,1)S(1)}, bf16[128,2048]{1,0:T(8,128)(2,1)}, u32[]{:S(2)}) copy-start(bf16[128,2048]{1,0:T(8,128)(2,1)} %param.10) | copy-start | bytes 1572868
  25.7 92.3 %all-to-all-start = ((bf16[16,64,2048]{2,1,0:T(8,128)(2,1)}), bf16[16,64,2048]{2,1,0:T(8,128)(2,1)}, u32[]{:S(2)}, u32[]{:S(2)}) async-start(bf16[16,64,2048]{2,1,0:T(8,128)(2,1)} %bitcast.137), calls=%async_computation | async-start | bytes 8388608 | tf_op jit(solution)/shard_map/all_to_all | solution.py:71
  118.0 97.7 %all-to-all-start.1 = ((bf16[16,64,2048]{2,1,0:T(8,128)(2,1)}), bf16[16,64,2048]{2,1,0:T(8,128)(2,1)}, u32[]{:S(2)}, u32[]{:S(2)}) async-start(bf16[16,64,2048]{2,1,0:T(8,128)(2,1)} %fusion), calls=%async_computation.1 | async-start | bytes 8388608 | tf_op jit(solution)/shard_map/all_to_all | solution.py:86
  132.9 6.3 %copy-start.2 = (bf16[1,2048,384]{2,1,0:T(8,128)(2,1)S(1)}, bf16[1,2048,384]{2,1,0:T(8,128)(2,1)}, u32[]{:S(2)}) copy-start(bf16[1,2048,384]{2,1,0:T(8,128)(2,1)} %param.11) | copy-start | bytes 4718596
  221.7 14.1 %copy-start.8 = (bf16[1024,384]{1,0:T(8,128)(2,1)}, bf16[1024,384]{1,0:T(8,128)(2,1)S(1)}, u32[]{:S(2)}) copy-start(bf16[1024,384]{1,0:T(8,128)(2,1)S(1)} %get-tuple-element.26) | copy-start | bytes 2359300
  235.8 4.5 copy-start.3
  244.7 251.9 %all-to-all-start.2 = ((bf16[16,64,2048]{2,1,0:T(8,128)(2,1)}), bf16[16,64,2048]{2,1,0:T(8,128)(2,1)}, u32[]{:S(2)}, u32[]{:S(2)}) async-start(bf16[16,64,2048]{2,1,0:T(8,128)(2,1)} %bitcast.136), calls=%async_computation.2 | async-start | bytes 8388608 | tf_op jit(solution)/shard_map/all_to_all | solution.py:104
  259.6 254.4 %all-reduce.5.cloned.1.call-start = ((), (), s32[]{:S(2)}) async-start(), calls=%async_computation.3 | async-start | bytes 9437184 | tf_op jit(solution)/shard_map/psum | solution.py:114
  259.7 14.4 %copy-start.9 = (bf16[1024,384]{1,0:T(8,128)(2,1)S(1)}, bf16[1024,384]{1,0:T(8,128)(2,1)}, u32[]{:S(2)}) copy-start(bf16[1024,384]{1,0:T(8,128)(2,1)} %copy-done.8) | copy-start | bytes 2359300
  263.2 207.6 %collective-permute-start.14 = (bf16[1,64,2048]{2,1,0:T(8,128)(2,1)S(1)}, bf16[1,64,2048]{2,1,0:T(8,128)(2,1)}, u32[]{:S(2)}, u32[]{:S(2)}) collective-permute-start(bf16[1,64,2048]{2,1,0:T(8,128)(2,1)S(1)} %get-tuple-element.8), channel_id=1, source_target_pairs={{0,15},{1,14},{2,13},{3,12},{4,11},{5,10},{6,9},{7,8},{8,7},{9,6},... | collective-permute-start | bytes 786440 | tf_op jit(solution)/shard_map/ppermute | solution.py:28
  267.4 201.7 %collective-permute-start.13 = (bf16[1,64,2048]{2,1,0:T(8,128)(2,1)S(1)}, bf16[1,64,2048]{2,1,0:T(8,128)(2,1)}, u32[]{:S(2)}, u32[]{:S(2)}) collective-permute-start(bf16[1,64,2048]{2,1,0:T(8,128)(2,1)S(1)} %get-tuple-element.9), channel_id=1, source_target_pairs={{0,14},{1,15},{2,12},{3,13},{4,10},{5,11},{6,8},{7,9},{8,6},{9,7},... | collective-permute-start | bytes 786440 | tf_op jit(solution)/shard_map/ppermute | solution.py:28
  268.8 198.6 %collective-permute-start.12 = (bf16[1,64,2048]{2,1,0:T(8,128)(2,1)S(1)}, bf16[1,64,2048]{2,1,0:T(8,128)(2,1)}, u32[]{:S(2)}, u32[]{:S(2)}) collective-permute-start(bf16[1,64,2048]{2,1,0:T(8,128)(2,1)S(1)} %get-tuple-element.10), channel_id=1, source_target_pairs={{0,13},{1,12},{2,15},{3,14},{4,9},{5,8},{6,11},{7,10},{8,5},{9,4},... | collective-permute-start | bytes 786440 | tf_op jit(solution)/shard_map/ppermute | solution.py:28
  272.1 193.7 %collective-permute-start.11 = (bf16[1,64,2048]{2,1,0:T(8,128)(2,1)S(1)}, bf16[1,64,2048]{2,1,0:T(8,128)(2,1)}, u32[]{:S(2)}, u32[]{:S(2)}) collective-permute-start(bf16[1,64,2048]{2,1,0:T(8,128)(2,1)S(1)} %get-tuple-element.11), channel_id=1, source_target_pairs={{0,12},{1,13},{2,14},{3,15},{4,8},{5,9},{6,10},{7,11},{8,4},{9,5},... | collective-permute-start | bytes 786440 | tf_op jit(solution)/shard_map/ppermute | solution.py:28
  272.6 7.0 %collective-permute-start = (bf16[1,64,2048]{2,1,0:T(8,128)(2,1)}, bf16[1,64,2048]{2,1,0:T(8,128)(2,1)}, u32[]{:S(2)}, u32[]{:S(2)}) collective-permute-start(bf16[1,64,2048]{2,1,0:T(8,128)(2,1)} %get-tuple-element.22), channel_id=1, source_target_pairs={{0,1},{1,0},{2,3},{3,2},{4,5},{5,4},{6,7},{7,6},{8,9},{9,8},{10,11... | collective-permute-start | bytes 786440 | tf_op jit(solution)/shard_map/ppermute | solution.py:28
  279.7 11.0 %collective-permute-start.1 = (bf16[1,64,2048]{2,1,0:T(8,128)(2,1)}, bf16[1,64,2048]{2,1,0:T(8,128)(2,1)S(1)}, u32[]{:S(2)}, u32[]{:S(2)}) collective-permute-start(bf16[1,64,2048]{2,1,0:T(8,128)(2,1)} %get-tuple-element.21), channel_id=1, source_target_pairs={{0,2},{1,3},{2,0},{3,1},{4,6},{5,7},{6,4},{7,5},{8,10},{9,11},{10,... | collective-permute-start | bytes 786440 | tf_op jit(solution)/shard_map/ppermute | solution.py:28
  290.7 30.8 %collective-permute-start.2 = (bf16[1,64,2048]{2,1,0:T(8,128)(2,1)S(1)}, bf16[1,64,2048]{2,1,0:T(8,128)(2,1)S(1)}, u32[]{:S(2)}, u32[]{:S(2)}) collective-permute-start(bf16[1,64,2048]{2,1,0:T(8,128)(2,1)S(1)} %get-tuple-element.20), channel_id=1, source_target_pairs={{0,3},{1,2},{2,1},{3,0},{4,7},{5,6},{6,5},{7,4},{8,11},{9,10},{10,... | collective-permute-start | bytes 786440 | tf_op jit(solution)/shard_map/ppermute | solution.py:28
  321.5 47.7 %collective-permute-start.3 = (bf16[1,64,2048]{2,1,0:T(8,128)(2,1)S(1)}, bf16[1,64,2048]{2,1,0:T(8,128)(2,1)S(1)}, u32[]{:S(2)}, u32[]{:S(2)}) collective-permute-start(bf16[1,64,2048]{2,1,0:T(8,128)(2,1)S(1)} %get-tuple-element.19), channel_id=1, source_target_pairs={{0,4},{1,5},{2,6},{3,7},{4,0},{5,1},{6,2},{7,3},{8,12},{9,13},{10,... | collective-permute-start | bytes 786440 | tf_op jit(solution)/shard_map/ppermute | solution.py:28
  369.2 7.9 %collective-permute-start.4 = (bf16[1,64,2048]{2,1,0:T(8,128)(2,1)S(1)}, bf16[1,64,2048]{2,1,0:T(8,128)(2,1)S(1)}, u32[]{:S(2)}, u32[]{:S(2)}) collective-permute-start(bf16[1,64,2048]{2,1,0:T(8,128)(2,1)S(1)} %get-tuple-element.18), channel_id=1, source_target_pairs={{0,5},{1,4},{2,7},{3,6},{4,1},{5,0},{6,3},{7,2},{8,13},{9,12},{10,... | collective-permute-start | bytes 786440 | tf_op jit(solution)/shard_map/ppermute | solution.py:28
  377.1 10.5 %collective-permute-start.5 = (bf16[1,64,2048]{2,1,0:T(8,128)(2,1)S(1)}, bf16[1,64,2048]{2,1,0:T(8,128)(2,1)S(1)}, u32[]{:S(2)}, u32[]{:S(2)}) collective-permute-start(bf16[1,64,2048]{2,1,0:T(8,128)(2,1)S(1)} %get-tuple-element.17), channel_id=1, source_target_pairs={{0,6},{1,7},{2,4},{3,5},{4,2},{5,3},{6,0},{7,1},{8,14},{9,15},{10,... | collective-permute-start | bytes 786440 | tf_op jit(solution)/shard_map/ppermute | solution.py:28
  387.6 8.2 %collective-permute-start.6 = (bf16[1,64,2048]{2,1,0:T(8,128)(2,1)S(1)}, bf16[1,64,2048]{2,1,0:T(8,128)(2,1)S(1)}, u32[]{:S(2)}, u32[]{:S(2)}) collective-permute-start(bf16[1,64,2048]{2,1,0:T(8,128)(2,1)S(1)} %get-tuple-element.16), channel_id=1, source_target_pairs={{0,7},{1,6},{2,5},{3,4},{4,3},{5,2},{6,1},{7,0},{8,15},{9,14},{10,... | collective-permute-start | bytes 786440 | tf_op jit(solution)/shard_map/ppermute | solution.py:28
  395.8 37.7 %collective-permute-start.7 = (bf16[1,64,2048]{2,1,0:T(8,128)(2,1)S(1)}, bf16[1,64,2048]{2,1,0:T(8,128)(2,1)S(1)}, u32[]{:S(2)}, u32[]{:S(2)}) collective-permute-start(bf16[1,64,2048]{2,1,0:T(8,128)(2,1)S(1)} %get-tuple-element.15), channel_id=1, source_target_pairs={{0,8},{1,9},{2,10},{3,11},{4,12},{5,13},{6,14},{7,15},{8,0},{9,1},... | collective-permute-start | bytes 786440 | tf_op jit(solution)/shard_map/ppermute | solution.py:28
  433.5 11.5 %collective-permute-start.8 = (bf16[1,64,2048]{2,1,0:T(8,128)(2,1)S(1)}, bf16[1,64,2048]{2,1,0:T(8,128)(2,1)S(1)}, u32[]{:S(2)}, u32[]{:S(2)}) collective-permute-start(bf16[1,64,2048]{2,1,0:T(8,128)(2,1)S(1)} %get-tuple-element.14), channel_id=1, source_target_pairs={{0,9},{1,8},{2,11},{3,10},{4,13},{5,12},{6,15},{7,14},{8,1},{9,0},... | collective-permute-start | bytes 786440 | tf_op jit(solution)/shard_map/ppermute | solution.py:28
  444.9 10.0 %collective-permute-start.9 = (bf16[1,64,2048]{2,1,0:T(8,128)(2,1)S(1)}, bf16[1,64,2048]{2,1,0:T(8,128)(2,1)S(1)}, u32[]{:S(2)}, u32[]{:S(2)}) collective-permute-start(bf16[1,64,2048]{2,1,0:T(8,128)(2,1)S(1)} %get-tuple-element.13), channel_id=1, source_target_pairs={{0,10},{1,11},{2,8},{3,9},{4,14},{5,15},{6,12},{7,13},{8,2},{9,3},... | collective-permute-start | bytes 786440 | tf_op jit(solution)/shard_map/ppermute | solution.py:28
  455.0 10.1 %collective-permute-start.10 = (bf16[1,64,2048]{2,1,0:T(8,128)(2,1)S(1)}, bf16[1,64,2048]{2,1,0:T(8,128)(2,1)S(1)}, u32[]{:S(2)}, u32[]{:S(2)}) collective-permute-start(bf16[1,64,2048]{2,1,0:T(8,128)(2,1)S(1)} %get-tuple-element.12), channel_id=1, source_target_pairs={{0,11},{1,10},{2,9},{3,8},{4,15},{5,14},{6,13},{7,12},{8,3},{9,2},... | collective-permute-start | bytes 786440 | tf_op jit(solution)/shard_map/ppermute | solution.py:28
  514.0 2.9 copy-start.5
  514.0 4.0 copy-start.4
  514.0 5.2 copy-start.1
Sparse Core Ops, SparseCore 0:
  279.4 29.5 all-reduce.4
